TPU v7x, 256 devices: a whole 4x4x8 slice. The times are simulated.
256 devices in a mesh: cg: 16 (over z, x_lo), vg: 16 (over x_hi, y, core).
Axes of the slice: x: 4 (x_hi: 2, x_lo: 2; x = x_hi * 2 + x_lo), y: 4, z: 8, core: 2. Of those that a mesh axis runs over, the one named last changes fastest.
Arguments:
- con_embed: float32 [262144, 128], P(('cg', 'vg')), may hold values from -6 to 6
- var_embed: float32 [262144, 128], P(('vg', 'cg')), may hold values from -6 to 6
- row_coef: float32 [262144], P(('cg', 'vg')), may hold values from 0.3 to 3
- col_coef: float32 [262144], P(('vg', 'cg')), may hold values from 0.3 to 3
- self_weight: float32 [128, 128], replicated, may hold values from -0.5 to 0.5
- msg_weight: float32 [128, 128], replicated, may hold values from -0.0234375 to 0.0234375
- timestep: int32 [1], replicated, may hold values from 0 to 999
- tile_rows: int32 [16, 16, 16], P('cg', 'vg'), may hold values from 0 to 31, as said below
- tile_cols: int32 [16, 16, 16], P('cg', 'vg'), may hold values from 0 to 31, as said below
- pattern: bfloat16 [16, 16, 16, 512, 512], P('cg', 'vg'), may hold values from -6 to 6
- cotangent: float32 [262144, 128], P(('cg', 'vg')), may hold values from -6 to 6
Outputs:
- con_update: float32 [262144, 128], P(('cg', 'vg'))
- grad_con: float32 [262144, 128], P(('cg', 'vg'))
- grad_var: float32 [262144, 128], P(('vg', 'cg'))
- grad_msg: float32 [128, 128], replicated
- grad_self: float32 [128, 128], replicated
Inputs may be any that keep to these rules, and one draw needn't show every extreme that they name: `tile_rows`: every device lists tile row 0 and tile row 31; a device lists distinct tiles unless 16 exceeds 32 * 32, and repeated tiles add. `tile_cols`: every device lists tile column 0 and tile column 31, together with the rows above: tiles (0, 0) and (31, 31) are on every list.
All inputs are finite; a program needn't handle non-finite values.
Results may differ from a plain program's by a relative error of at most 0.007.
Values may be sent and summed in bfloat16 or wider, within the bound.
No kernel may reach another device: no remote copies, remote signals or barrier semaphores. Data moves between devices by JAX's collectives and lax.ppermute only.
A program may use at most 128 MiB of HBM per device.

v0:
```python
import math
import jax
import jax.numpy as jnp
from jax import lax
from jax.sharding import PartitionSpec as P

H = 128
TB = 512


def body(
    con_embed,
    var_embed,
    row_coef,
    col_coef,
    self_weight,
    msg_weight,
    timestep,
    tile_rows,
    tile_cols,
    pattern,
    cotangent,
):
    highest = lax.Precision.HIGHEST
    con_count = con_embed.shape[0]
    var_count = var_embed.shape[0]
    row_blocks = con_count * lax.axis_size("vg") // TB
    col_blocks = var_count * lax.axis_size("cg") // TB
    row_index = tile_rows.reshape(-1)
    col_index = tile_cols.reshape(-1)
    tile_count = row_index.shape[0]
    per_turn = math.gcd(tile_count, 8)
    turns = tile_count // per_turn
    patterns_here = pattern.reshape(turns, per_turn, TB, TB)
    row_turns = row_index.reshape(turns, per_turn)
    col_turns = col_index.reshape(turns, per_turn)
    gathered, scales = (
        lax.all_gather(var_embed, "cg", axis=0, tiled=True),
        lax.all_gather(col_coef, "cg", axis=0, tiled=True),
    )
    projected = (
        jnp.dot(gathered, msg_weight, precision=highest, preferred_element_type=jnp.float32)
        * scales[:, None]
    ).astype(jnp.bfloat16)
    source_blocks = projected.reshape(col_blocks, TB, H)
    row_ids = jnp.arange(row_blocks, dtype=jnp.int32)
    col_ids = jnp.arange(col_blocks, dtype=jnp.int32)

    def forward_turn(running, inputs):
        rows_now, cols_now, tile_mask = inputs
        products = jnp.einsum(
            "grc,gch->grh", tile_mask, source_blocks[cols_now], preferred_element_type=jnp.float32
        )
        selector = (rows_now[None, :] == row_ids[:, None]).astype(jnp.float32)
        running = running + jnp.dot(
            selector,
            products.reshape(per_turn, TB * H),
            precision=highest,
            preferred_element_type=jnp.float32,
        )
        return (running, None)

    forward_sum, _ = lax.scan(
        forward_turn,
        jnp.zeros((row_blocks, TB * H), jnp.float32),
        (row_turns, col_turns, patterns_here),
    )
    messages = lax.psum_scatter(
        forward_sum.reshape(row_blocks * TB, H), "vg", scatter_dimension=0, tiled=True
    )
    frequency = jnp.exp(-math.log(10000.0) * jnp.arange(H // 2, dtype=jnp.float32) / (H // 2))
    phases = timestep[0].astype(jnp.float32) * frequency
    time_embed = jnp.concatenate([jnp.sin(phases), jnp.cos(phases)])
    preact = (
        jnp.dot(con_embed, self_weight, precision=highest, preferred_element_type=jnp.float32)
        + row_coef[:, None] * messages
        + time_embed[None, :]
    )
    sigmoid_z = jax.nn.sigmoid(preact)
    con_update = con_embed + preact * sigmoid_z
    grad_pre = cotangent * sigmoid_z * (1.0 + preact * (1.0 - sigmoid_z))
    grad_con = cotangent + jnp.dot(
        grad_pre, self_weight.T, precision=highest, preferred_element_type=jnp.float32
    )
    local_self = jnp.dot(
        con_embed.T, grad_pre, precision=highest, preferred_element_type=jnp.float32
    )
    grad_messages = (row_coef[:, None] * grad_pre).astype(jnp.bfloat16)
    whole_rows = lax.all_gather(grad_messages, "vg", axis=0, tiled=True).reshape(row_blocks, TB, H)

    def backward_turn(running, inputs):
        rows_now, cols_now, tile_mask = inputs
        products = jnp.einsum(
            "grc,grh->gch", tile_mask, whole_rows[rows_now], preferred_element_type=jnp.float32
        )
        selector = (cols_now[None, :] == col_ids[:, None]).astype(jnp.float32)
        running = running + jnp.dot(
            selector,
            products.reshape(per_turn, TB * H),
            precision=highest,
            preferred_element_type=jnp.float32,
        )
        return (running, None)

    backward_sum, _ = lax.scan(
        backward_turn,
        jnp.zeros((col_blocks, TB * H), jnp.float32),
        (row_turns, col_turns, patterns_here),
    )
    grad_projected = lax.psum_scatter(
        backward_sum.reshape(col_blocks * TB, H), "cg", scatter_dimension=0, tiled=True
    )
    grad_lin = col_coef[:, None] * grad_projected
    grad_var = jnp.dot(
        grad_lin, msg_weight.T, precision=highest, preferred_element_type=jnp.float32
    )
    local_msg = jnp.dot(
        var_embed.T, grad_lin, precision=highest, preferred_element_type=jnp.float32
    )
    grad_msg, grad_self = lax.psum((local_msg, local_self), ("cg", "vg"))
    return (con_update, grad_con, grad_var, grad_msg, grad_self)


def solution(mesh):
    in_specs = (
        P(("cg", "vg"), None),
        P(("vg", "cg"), None),
        P(("cg", "vg")),
        P(("vg", "cg")),
        P(),
        P(),
        P(),
        P("cg", "vg", None),
        P("cg", "vg", None),
        P("cg", "vg", None, None, None),
        P(("cg", "vg"), None),
    )
    out_specs = (P(("cg", "vg"), None), P(("cg", "vg"), None), P(("vg", "cg"), None), P(), P())
    return jax.shard_map(body, mesh=mesh, in_specs=in_specs, out_specs=out_specs, check_vma=False)
```

profile of v0, /device:TPU:2, one launch (start us, length us, event | category | flops | bytes accessed | tf_op | source)
XLA Modules:
  0.0 902.7 jit_solution(3706184754790364743)
XLA Ops:
  7.2 0.0 copy-start
  7.2 0.0 all-gather.3.cloned.1.call-start
  7.2 0.7 all-gather.3.cloned.1.call-update
  7.9 0.0 reduce-scatter.3.cloned.1.call-start
  8.0 0.5 broadcast.96
  8.5 1.3 reduce.6
  9.8 0.1 reshape_reshape.6
  9.9 1.3 reduce.7
  11.2 0.1 reshape_reshape.7
  11.3 37.0 %all_gather.10 = f32[16384]{0:T(1024)S(1)} all-gather(f32[1024]{0:T(1024)} %param.18), channel_id=1, replica_groups=mesh['cg'=16,'vg'=16] {'cg'}, dimensions={0}, use_global_device_ids=true | all-gather | bytes 69632 | tf_op jit(solution)/shard_map/all_gather | solution.py:39
  48.3 146.8 %all-gather.3.cloned.1.call-done = f32[16384,128]{1,0:T(8,128)} async-done(((f32[1024,128]{1,0:T(8,128)}), f32[16384,128]{1,0:T(8,128)}) %all-gather.3.cloned.1.call-update) | async-done | bytes 8388624 | tf_op jit(solution)/shard_map/all_gather | solution.py:38
  195.1 0.0 copy-done
  195.1 18.7 %fusion.30 = bf16[16384,128]{1,0:T(8,128)(2,1)} fusion(f32[16384,128]{1,0:T(8,128)} %all-gather.3.cloned.1.call-done, f32[128,128]{1,0:T(8,128)S(1)} %copy-done, f32[16384]{0:T(1024)S(1)} %all_gather.10), kind=kOutput, calls=%fused_computation.39 | convolution fusion | flops 3225419776 | bytes 12713984 | tf_op jit(solution)/shard_map/dot_general | solution.py:42
  213.8 30.1 %while.22 = (s32[]{:T(128)}, f32[32,65536]{1,0:T(8,128)}, s32[2,8]{1,0:T(2,128)S(1)}, bf16[2,8,512,512]{3,2,1,0:T(8,128)(2,1)}, s32[2,8]{1,0:T(2,128)S(1)}, /*in...) while((s32[]{:T(128)}, f32[32,65536]{1,0:T(8,128)}, s32[2,8]{1,0:T(2,128)S(1)}, ...), condition=%wide.region_1.2_spmd.clone, body=%wide.region_0.1_spmd.clone.sunk | while | flops 742393088 | bytes 28316484 | solution.py:63
  213.8 2.9 gather_fusion
  216.7 3.4 fusion.65
  220.2 7.5 convolution_add_fusion.6
  227.7 2.9 gather_fusion
  230.7 3.4 fusion.65
  234.1 9.7 %convolution_add_fusion.6 = f32[32,65536]{1,0:T(8,128)} fusion(f32[32,65536]{1,0:T(8,128)} %get-tuple-element.263, pred[]{:T(512)S(6)} %compare.6, f32[1,8,512,128]{3,2,1,0:T(8,128)S(1)} %fusion.65, s32[8]{0:T(128)S(1)} %fusion.66), kind=kOutput, calls=%fused_computation.4.clone.1 | convolution fusion | flops 205521152 | bytes 18874400 | tf_op jit(solution)/shard_map/while/body/eval_jaxpr/dot_general | solution.py:55
  243.8 7.3 reshape.96
  251.1 0.0 copy-start.3
  251.1 0.0 copy-start.5
  251.1 0.0 copy-start.7
  251.1 0.0 copy-start.8
  251.2 0.0 reduce-scatter.3.cloned.1.call-update
  251.2 0.0 all-gather.5.cloned.1.call-start
  252.0 0.1 pad_maximum_fusion
  252.1 110.5 %reduce-scatter.3.cloned.1.call-done = f32[1024,128]{1,0:T(8,128)} async-done(((f32[16384,128]{1,0:T(8,128)}), f32[1024,128]{1,0:T(8,128)}) %reduce-scatter.3.cloned.1.call-update) | async-done | bytes 524304 | tf_op jit(solution)/shard_map/reduce_scatter | solution.py:68
  362.6 0.0 copy-done.3
  362.6 0.0 copy-done.5
  362.6 0.0 copy-done.7
  362.6 0.0 copy-done.8
  362.6 2.9 multiply_convert_fusion
  365.4 0.0 all-gather.5.cloned.1.call-update
  365.5 0.2 reduce-scatter.5.cloned.1.call-start
  365.7 12.4 %copy.20 = bf16[1,1,16,512,512]{3,4,2,1,0:T(8,128)(2,1)} copy(bf16[1,1,16,512,512]{4,3,2,1,0:T(8,128)(2,1)} %bitcast.88) | data formatting | bytes 16777216 | tf_op args[9]
  378.0 47.1 %all-gather.5.cloned.1.call-done = bf16[16384,128]{1,0:T(8,128)(2,1)} async-done(((bf16[1024,128]{1,0:T(8,128)(2,1)}), bf16[16384,128]{1,0:T(8,128)(2,1)}) %all-gather.5.cloned.1.call-update) | async-done | bytes 4194320 | tf_op jit(solution)/shard_map/all_gather | solution.py:89
  425.2 29.9 %while.23 = (s32[]{:T(128)}, f32[32,65536]{1,0:T(8,128)}, s32[2,8]{1,0:T(2,128)S(1)}, bf16[2,8,512,512]{2,3,1,0:T(8,128)(2,1)}, s32[2,8]{1,0:T(2,128)S(1)}, /*in...) while((s32[]{:T(128)}, f32[32,65536]{1,0:T(8,128)}, s32[2,8]{1,0:T(2,128)S(1)}, ...), condition=%wide.region_4.5_spmd.clone, body=%wide.region_3.4_spmd.clone.sunk | while | flops 742393088 | bytes 28316484 | solution.py:105
  425.2 2.9 gather_fusion.1
  428.1 3.4 fusion.71
  431.6 7.4 convolution_add_fusion.7
  439.0 2.9 gather_fusion.1
  442.0 3.4 fusion.71
  445.4 9.6 %convolution_add_fusion.7 = f32[32,65536]{1,0:T(8,128)} fusion(f32[32,65536]{1,0:T(8,128)} %get-tuple-element.287, pred[]{:T(512)S(6)} %compare.7, f32[1,8,512,128]{3,2,1,0:T(8,128)S(1)} %fusion.71, s32[8]{0:T(128)S(1)} %fusion.72), kind=kOutput, calls=%fused_computation.21.clone.1 | convolution fusion | flops 205521152 | bytes 18874400 | tf_op jit(solution)/shard_map/while/body/eval_jaxpr/dot_general | solution.py:97
  455.0 7.4 reshape.98
  462.4 0.0 copy-start.4
  462.4 0.0 copy-start.2
  462.5 0.0 reduce-scatter.5.cloned.1.call-update
  462.5 0.0 all-reduce.3.cloned.1.call-start
  462.5 0.9 copy-done.4
  463.5 0.2 copy-done.6
  463.6 0.2 copy-done.9
  463.8 1.7 convolution_bitcast_fusion
  465.5 1.5 convolution_add_fusion.2
  467.1 175.9 %reduce-scatter.5.cloned.1.call-done = f32[1024,128]{1,0:T(8,128)} async-done(((f32[16384,128]{1,0:T(8,128)}), f32[1024,128]{1,0:T(8,128)}) %reduce-scatter.5.cloned.1.call-update) | async-done | bytes 524304 | tf_op jit(solution)/shard_map/reduce_scatter | solution.py:110
  643.0 0.0 copy-done.1
  643.0 0.0 copy-done.2
  643.0 2.8 convolution_bitcast_fusion.1
  645.8 0.0 all-reduce.3.cloned.1.call-update
  645.8 2.5 fusion.33
  648.3 244.7 %all-reduce.3.cloned.1.call-done = (f32[128,128]{0,1:T(8,128)}, f32[128,128]{0,1:T(8,128)}) async-done(((f32[128,128]{0,1:T(8,128)}, f32[128,128]{0,1:T(8,128)}), (f32[128,128]{0,1:T(8,128)}, f32[128,128]{0,1:T(8,128)})) %all-reduce.3.cloned.1.call-update) | async-done | bytes 131088 | tf_op jit(solution)/shard_map/psum | solution.py:120
  893.0 1.6 copy.22
  894.6 1.6 copy.23
  (18 shorter events, 0.2 us)
Async XLA Ops:
  7.2 187.9 %copy-start = (f32[128,128]{1,0:T(8,128)S(1)}, f32[128,128]{1,0:T(8,128)}, u32[]{:S(2)}) copy-start(f32[128,128]{1,0:T(8,128)} %param.20) | copy-start | bytes 196612
  7.2 187.9 %all-gather.3.cloned.1.call-start = ((), (), s32[]{:S(2)}) async-start(), calls=%async_computation.2 | async-start | bytes 8912896 | tf_op jit(solution)/shard_map/all_gather | solution.py:38
  7.9 354.7 %reduce-scatter.3.cloned.1.call-start = ((), (), s32[]{:S(2)}) async-start(), calls=%async_computation.3 | async-start | bytes 8912896 | tf_op jit(solution)/shard_map/reduce_scatter | solution.py:68
  251.1 111.4 %copy-start.3 = (f32[1024,128]{1,0:T(8,128)S(1)}, f32[1024,128]{1,0:T(8,128)}, u32[]{:S(2)}) copy-start(f32[1024,128]{1,0:T(8,128)} %param.15) | copy-start | bytes 1572868
  251.1 111.4 %copy-start.5 = (f32[1024,128]{1,0:T(8,128)S(1)}, f32[1024,128]{1,0:T(8,128)}, u32[]{:S(2)}) copy-start(f32[1024,128]{1,0:T(8,128)} %param.25) | copy-start | bytes 1572868
  251.1 111.4 %copy-start.7 = (f32[128,128]{1,0:T(8,128)S(1)}, f32[128,128]{1,0:T(8,128)}, u32[]{:S(2)}) copy-start(f32[128,128]{1,0:T(8,128)} %param.19) | copy-start | bytes 196612
  251.1 111.4 %copy-start.8 = (f32[1024]{0:T(1024)S(1)}, f32[1024]{0:T(1024)}, u32[]{:S(2)}) copy-start(f32[1024]{0:T(1024)} %param.17) | copy-start | bytes 12292
  251.2 174.0 %all-gather.5.cloned.1.call-start = ((), (), s32[]{:S(2)}) async-start(), calls=%async_computation.4 | async-start | bytes 4456448 | tf_op jit(solution)/shard_map/all_gather | solution.py:89
  365.5 277.5 %reduce-scatter.5.cloned.1.call-start = ((), (), s32[]{:S(2)}) async-start(), calls=%async_computation.5 | async-start | bytes 8912896 | tf_op jit(solution)/shard_map/reduce_scatter | solution.py:110
  462.4 1.0 copy-start.4
  462.4 1.2 copy-start.6
  462.4 1.4 copy-start.9
  462.4 180.5 %copy-start.1 = (f32[1024,128]{1,0:T(8,128)S(1)}, f32[1024,128]{1,0:T(8,128)}, u32[]{:S(2)}) copy-start(f32[1024,128]{1,0:T(8,128)} %param.16) | copy-start | bytes 1572868
  462.4 180.5 %copy-start.2 = (f32[1024]{0:T(1024)S(1)}, f32[1024]{0:T(1024)}, u32[]{:S(2)}) copy-start(f32[1024]{0:T(1024)} %param.18) | copy-start | bytes 12292
  462.5 430.6 %all-reduce.3.cloned.1.call-start = ((), (), s32[]{:S(2)}) async-start(), calls=%async_computation.6 | async-start | bytes 262144 | tf_op jit(solution)/shard_map/psum | solution.py:120
Sparse Core Ops, SparseCore 0:
  9.8 185.2 all-gather.2
  251.3 111.2 reduce-scatter.2
  365.9 59.2 all-gather.4
  462.6 180.3 reduce-scatter.4
  649.0 244.0 all-reduce.2
where the time goes:
time: 904 us; the launch traced here: 903 us
  waiting for transfers between devices  726 us (80%)
  matrix products  78.1 us (9%)
  local copies, waits for them, and re-layouts  44 us (5%)
  blocking collectives  37 us (4%)
  between operations  14.6 us (2%)
    psum x1, waiting for transfers between devices, body(): grad_msg, grad_self = lax.psum((local_msg, local_self), ('cg', 'vg'))  245 us
    reduce_scatter x1, waiting for transfers between devices, body(): lax.psum_scatter(backward_sum.reshape(col_blocks * TB, H), 'cg', scatter_...  176 us
    all_gather x1, waiting for transfers between devices, body(): lax.all_gather(var_embed, 'cg', axis=0, tiled=True)  147 us
    reduce_scatter x1, waiting for transfers between devices, body(): lax.psum_scatter(forward_sum.reshape(row_blocks * TB, H), 'vg', scatter_d...  110 us
    all_gather x1, waiting for transfers between devices, body(): lax.all_gather(grad_messages, 'vg', axis=0, tiled=True)  47.1 us
    all_gather x1, blocking collectives, body(): lax.all_gather(col_coef, 'cg', axis=0, tiled=True)  37 us
    dot_general x1, matrix products, body(): jnp.dot(gathered, msg_weight, precision=highest, preferred_element_type=j...  18.7 us
  transfers between devices with their start and end apart: 5, of which 5 were waited for; matrix products, arithmetic and copies ran while one was open for 2% of the time, Pallas kernels for 0%

commit v1 on v0

--- a/solution.py
+++ b/solution.py
@@ -1,11 +1,21 @@
+import functools
 import math
 import jax
 import jax.numpy as jnp
 from jax import lax
 from jax.sharding import PartitionSpec as P
+from jax.lax import psum
 
 H = 128
 TB = 512
+
+
+def press_the_object(xx, axis_tag, mesh_ax):
+    before = psum(xx, axis_tag)
+    return psum(before, mesh_ax)
+
+
+pass_the_sheet = functools.partial(press_the_object, axis_tag="cg", mesh_ax="vg")
 
 
 def body(
@@ -117,7 +127,7 @@
     local_msg = jnp.dot(
         var_embed.T, grad_lin, precision=highest, preferred_element_type=jnp.float32
     )
-    grad_msg, grad_self = lax.psum((local_msg, local_self), ("cg", "vg"))
+    grad_msg, grad_self = pass_the_sheet((local_msg, local_self))
     return (con_update, grad_con, grad_var, grad_msg, grad_self)
 
 

time: 904 us -> 940 us (1.040)
  waiting for transfers between devices: 726 us -> 760 us
    psum x1 -> x2, waiting for transfers between devices: 245 us -> 277 us  [the longest x1 142 us: press_the_object(): return psum(before, mesh_ax)]
  transfers between devices with their start and end apart: 5 -> 6, of which waited for: 5 -> 6; matrix products, arithmetic and copies ran while one was open for 2% -> 2% of each run, Pallas kernels for 0% -> 0%
where the time goes in v1:
time: 940 us; the launch traced here: 937 us
  waiting for transfers between devices  760 us (81%)
  matrix products  78.2 us (8%)
  local copies, waits for them, and re-layouts  43.9 us (5%)
  blocking collectives  37 us (4%)
  between operations  14.9 us (2%)
    reduce_scatter x1, waiting for transfers between devices, body(): lax.psum_scatter(backward_sum.reshape(col_blocks * TB, H), 'cg', scatter_...  177 us
    all_gather x1, waiting for transfers between devices, body(): lax.all_gather(var_embed, 'cg', axis=0, tiled=True)  147 us
    psum x1, waiting for transfers between devices, press_the_object(): return psum(before, mesh_ax)  142 us
    psum x1, waiting for transfers between devices, press_the_object(): before = psum(xx, axis_tag)  136 us
    reduce_scatter x1, waiting for transfers between devices, body(): lax.psum_scatter(forward_sum.reshape(row_blocks * TB, H), 'vg', scatter_d...  110 us
    all_gather x1, waiting for transfers between devices, body(): lax.all_gather(grad_messages, 'vg', axis=0, tiled=True)  47.2 us
    all_gather x1, blocking collectives, body(): lax.all_gather(col_coef, 'cg', axis=0, tiled=True)  37 us
  transfers between devices with their start and end apart: 6, of which 6 were waited for; matrix products, arithmetic and copies ran while one was open for 2% of the time, Pallas kernels for 0%

profile of v1, /device:TPU:2, one launch (start us, length us, event | category | flops | bytes accessed | tf_op | source)
XLA Modules:
  0.0 937.2 jit_solution(16485644198049491168)
XLA Ops:
  7.2 0.0 copy-start
  7.2 0.0 all-gather.3.cloned.1.call-start
  7.2 0.7 all-gather.3.cloned.1.call-update
  7.9 0.0 reduce-scatter.3.cloned.1.call-start
  8.0 0.5 broadcast.96
  8.5 1.3 reduce.6
  9.8 0.1 reshape_reshape.6
  9.9 1.3 reduce.7
  11.2 0.1 reshape_reshape.7
  11.3 37.0 %all_gather.10 = f32[16384]{0:T(1024)S(1)} all-gather(f32[1024]{0:T(1024)} %param.18), channel_id=1, replica_groups=mesh['cg'=16,'vg'=16] {'cg'}, dimensions={0}, use_global_device_ids=true | all-gather | bytes 69632 | tf_op jit(solution)/shard_map/all_gather | solution.py:49
  48.3 146.8 %all-gather.3.cloned.1.call-done = f32[16384,128]{1,0:T(8,128)} async-done(((f32[1024,128]{1,0:T(8,128)}), f32[16384,128]{1,0:T(8,128)}) %all-gather.3.cloned.1.call-update) | async-done | bytes 8388624 | tf_op jit(solution)/shard_map/all_gather | solution.py:48
  195.1 0.0 copy-done
  195.1 18.7 %fusion.30 = bf16[16384,128]{1,0:T(8,128)(2,1)} fusion(f32[16384,128]{1,0:T(8,128)} %all-gather.3.cloned.1.call-done, f32[128,128]{1,0:T(8,128)S(1)} %copy-done, f32[16384]{0:T(1024)S(1)} %all_gather.10), kind=kOutput, calls=%fused_computation.39 | convolution fusion | flops 3225419776 | bytes 12713984 | tf_op jit(solution)/shard_map/dot_general | solution.py:52
  213.7 30.1 %while.22 = (s32[]{:T(128)}, f32[32,65536]{1,0:T(8,128)}, s32[2,8]{1,0:T(2,128)S(1)}, bf16[2,8,512,512]{3,2,1,0:T(8,128)(2,1)}, s32[2,8]{1,0:T(2,128)S(1)}, /*in...) while((s32[]{:T(128)}, f32[32,65536]{1,0:T(8,128)}, s32[2,8]{1,0:T(2,128)S(1)}, ...), condition=%wide.region_1.2_spmd.clone, body=%wide.region_0.1_spmd.clone.sunk | while | flops 742393088 | bytes 28316484 | solution.py:73
  213.8 2.9 gather_fusion
  216.7 3.4 fusion.65
  220.2 7.6 convolution_add_fusion.6
  227.8 2.9 gather_fusion
  230.7 3.4 fusion.65
  234.2 9.7 %convolution_add_fusion.6 = f32[32,65536]{1,0:T(8,128)} fusion(f32[32,65536]{1,0:T(8,128)} %get-tuple-element.265, pred[]{:T(512)S(6)} %compare.6, f32[1,8,512,128]{3,2,1,0:T(8,128)S(1)} %fusion.65, s32[8]{0:T(128)S(1)} %fusion.66), kind=kOutput, calls=%fused_computation.4.clone.1 | convolution fusion | flops 205521152 | bytes 18874400 | tf_op jit(solution)/shard_map/while/body/eval_jaxpr/dot_general | solution.py:65
  243.9 7.3 reshape.96
  251.2 0.0 copy-start.3
  251.2 0.0 copy-start.5
  251.2 0.0 reduce-scatter.3.cloned.1.call-update
  251.2 0.0 all-gather.5.cloned.1.call-start
  252.1 0.1 pad_maximum_fusion
  252.2 110.4 %reduce-scatter.3.cloned.1.call-done = f32[1024,128]{1,0:T(8,128)} async-done(((f32[16384,128]{1,0:T(8,128)}), f32[1024,128]{1,0:T(8,128)}) %reduce-scatter.3.cloned.1.call-update) | async-done | bytes 524304 | tf_op jit(solution)/shard_map/reduce_scatter | solution.py:78
  362.6 0.0 copy-done.3
  362.6 0.0 copy-done.5
  362.6 0.0 copy-done.7
  362.6 0.0 copy-done.8
  362.6 2.8 multiply_convert_fusion
  365.4 0.0 all-gather.5.cloned.1.call-update
  365.5 0.2 reduce-scatter.5.cloned.1.call-start
  365.7 12.3 %copy.20 = bf16[1,1,16,512,512]{3,4,2,1,0:T(8,128)(2,1)} copy(bf16[1,1,16,512,512]{4,3,2,1,0:T(8,128)(2,1)} %bitcast.88) | data formatting | bytes 16777216 | tf_op args[9]
  378.0 47.2 %all-gather.5.cloned.1.call-done = bf16[16384,128]{1,0:T(8,128)(2,1)} async-done(((bf16[1024,128]{1,0:T(8,128)(2,1)}), bf16[16384,128]{1,0:T(8,128)(2,1)}) %all-gather.5.cloned.1.call-update) | async-done | bytes 4194320 | tf_op jit(solution)/shard_map/all_gather | solution.py:99
  425.2 30.0 %while.23 = (s32[]{:T(128)}, f32[32,65536]{1,0:T(8,128)}, s32[2,8]{1,0:T(2,128)S(1)}, bf16[2,8,512,512]{2,3,1,0:T(8,128)(2,1)}, s32[2,8]{1,0:T(2,128)S(1)}, /*in...) while((s32[]{:T(128)}, f32[32,65536]{1,0:T(8,128)}, s32[2,8]{1,0:T(2,128)S(1)}, ...), condition=%wide.region_4.5_spmd.clone, body=%wide.region_3.4_spmd.clone.sunk | while | flops 742393088 | bytes 28316484 | solution.py:115
  425.2 2.9 gather_fusion.1
  428.2 3.4 fusion.71
  431.6 7.5 convolution_add_fusion.7
  439.1 2.9 gather_fusion.1
  442.1 3.4 fusion.71
  445.5 9.6 %convolution_add_fusion.7 = f32[32,65536]{1,0:T(8,128)} fusion(f32[32,65536]{1,0:T(8,128)} %get-tuple-element.289, pred[]{:T(512)S(6)} %compare.7, f32[1,8,512,128]{3,2,1,0:T(8,128)S(1)} %fusion.71, s32[8]{0:T(128)S(1)} %fusion.72), kind=kOutput, calls=%fused_computation.21.clone.1 | convolution fusion | flops 205521152 | bytes 18874400 | tf_op jit(solution)/shard_map/while/body/eval_jaxpr/dot_general | solution.py:107
  455.2 7.4 reshape.98
  462.6 0.0 copy-start.2
  462.6 0.0 reduce-scatter.5.cloned.1.call-update
  462.6 0.0 all-reduce.7.cloned.1.call-start
  462.7 0.9 copy-done.4
  463.6 0.2 copy-done.6
  463.8 0.2 copy-done.9
  463.9 1.7 convolution_bitcast_fusion
  465.7 177.4 %reduce-scatter.5.cloned.1.call-done = f32[1024,128]{1,0:T(8,128)} async-done(((f32[16384,128]{1,0:T(8,128)}), f32[1024,128]{1,0:T(8,128)}) %reduce-scatter.5.cloned.1.call-update) | async-done | bytes 524304 | tf_op jit(solution)/shard_map/reduce_scatter | solution.py:120
  643.1 0.0 copy-done.1
  643.1 0.0 copy-done.2
  643.1 2.8 convolution_bitcast_fusion.1
  645.9 0.0 all-reduce.7.cloned.1.call-update
  646.0 0.0 all-reduce.5.cloned.1.call-start
  646.0 1.5 convolution_add_fusion.2
  647.5 135.5 %all-reduce.7.cloned.1.call-done = (f32[128,128]{0,1:T(8,128)}, f32[128,128]{0,1:T(8,128)}) async-done(((f32[128,128]{0,1:T(8,128)}, f32[128,128]{0,1:T(8,128)}), (f32[128,128]{0,1:T(8,128)}, f32[128,128]{0,1:T(8,128)})) %all-reduce.7.cloned.1.call-update) | async-done | bytes 131088 | tf_op jit(solution)/shard_map/psum | solution.py:14
  783.0 0.0 all-reduce.5.cloned.1.call-update
  783.1 2.5 fusion.33
  785.5 141.7 %all-reduce.5.cloned.1.call-done = (f32[128,128]{0,1:T(8,128)}, f32[128,128]{0,1:T(8,128)}) async-done(((f32[128,128]{0,1:T(8,128)}, f32[128,128]{0,1:T(8,128)}), (f32[128,128]{0,1:T(8,128)}, f32[128,128]{0,1:T(8,128)})) %all-reduce.5.cloned.1.call-update) | async-done | bytes 131088 | tf_op jit(solution)/shard_map/psum | solution.py:15
  927.2 1.6 copy.22
  928.8 1.6 copy.23
  (21 shorter events, 0.2 us)
Async XLA Ops:
  7.2 187.9 %copy-start = (f32[128,128]{1,0:T(8,128)S(1)}, f32[128,128]{1,0:T(8,128)}, u32[]{:S(2)}) copy-start(f32[128,128]{1,0:T(8,128)} %param.20) | copy-start | bytes 196612
  7.2 187.9 %all-gather.3.cloned.1.call-start = ((), (), s32[]{:S(2)}) async-start(), calls=%async_computation.2 | async-start | bytes 8912896 | tf_op jit(solution)/shard_map/all_gather | solution.py:48
  7.9 354.7 %reduce-scatter.3.cloned.1.call-start = ((), (), s32[]{:S(2)}) async-start(), calls=%async_computation.3 | async-start | bytes 8912896 | tf_op jit(solution)/shard_map/reduce_scatter | solution.py:78
  251.2 111.4 %copy-start.3 = (f32[1024,128]{1,0:T(8,128)S(1)}, f32[1024,128]{1,0:T(8,128)}, u32[]{:S(2)}) copy-start(f32[1024,128]{1,0:T(8,128)} %param.15) | copy-start | bytes 1572868
  251.2 111.4 %copy-start.5 = (f32[1024,128]{1,0:T(8,128)S(1)}, f32[1024,128]{1,0:T(8,128)}, u32[]{:S(2)}) copy-start(f32[1024,128]{1,0:T(8,128)} %param.25) | copy-start | bytes 1572868
  251.2 111.4 %copy-start.7 = (f32[128,128]{1,0:T(8,128)S(1)}, f32[128,128]{1,0:T(8,128)}, u32[]{:S(2)}) copy-start(f32[128,128]{1,0:T(8,128)} %param.19) | copy-start | bytes 196612
  251.2 111.4 %copy-start.8 = (f32[1024]{0:T(1024)S(1)}, f32[1024]{0:T(1024)}, u32[]{:S(2)}) copy-start(f32[1024]{0:T(1024)} %param.17) | copy-start | bytes 12292
  251.2 173.9 %all-gather.5.cloned.1.call-start = ((), (), s32[]{:S(2)}) async-start(), calls=%async_computation.4 | async-start | bytes 4456448 | tf_op jit(solution)/shard_map/all_gather | solution.py:99
  365.5 277.6 %reduce-scatter.5.cloned.1.call-start = ((), (), s32[]{:S(2)}) async-start(), calls=%async_computation.5 | async-start | bytes 8912896 | tf_op jit(solution)/shard_map/reduce_scatter | solution.py:120
  462.6 1.0 copy-start.4
  462.6 1.2 copy-start.6
  462.6 1.4 copy-start.9
  462.6 180.5 %copy-start.1 = (f32[1024,128]{1,0:T(8,128)S(1)}, f32[1024,128]{1,0:T(8,128)}, u32[]{:S(2)}) copy-start(f32[1024,128]{1,0:T(8,128)} %param.16) | copy-start | bytes 1572868
  462.6 180.5 %copy-start.2 = (f32[1024]{0:T(1024)S(1)}, f32[1024]{0:T(1024)}, u32[]{:S(2)}) copy-start(f32[1024]{0:T(1024)} %param.18) | copy-start | bytes 12292
  462.6 320.4 %all-reduce.7.cloned.1.call-start = ((), (), s32[]{:S(2)}) async-start(), calls=%async_computation.7 | async-start | bytes 262144 | tf_op jit(solution)/shard_map/psum | solution.py:14
  646.0 281.3 %all-reduce.5.cloned.1.call-start = ((), (), s32[]{:S(2)}) async-start(), calls=%async_computation.6 | async-start | bytes 262144 | tf_op jit(solution)/shard_map/psum | solution.py:15
Sparse Core Ops, SparseCore 0:
  9.8 185.2 all-gather.2
  251.4 111.1 reduce-scatter.2
  365.9 59.2 all-gather.4
  462.7 180.3 reduce-scatter.4
  646.2 136.8 all-reduce.6
  785.7 141.4 all-reduce.4
